TPU v7x, 256 devices: a whole 4x4x8 slice. The times are simulated.
256 devices in a mesh: dp: 16 (over y, x), cls: 16 (over z, core).
Axes of the slice: x: 4, y: 4, z: 8, core: 2. Of those that a mesh axis runs over, the one named last changes fastest.
Arguments:
- images: bfloat16 [16384, 64, 128], P(('dp', 'cls')), may hold values from -6 to 6
- references: bfloat16 [256, 64, 128], P('cls'), may hold values from -0.0625 to 0.0625
- ctf: float32 [128, 64], replicated, may hold values from -1 to 1
- class_ids: int32 [16384, 1], P(('dp', 'cls')), may hold values from 0 to 255
- rot_ids: int32 [16384], P(('dp', 'cls')), may hold values from 0 to 35
- group_ids: int32 [16384], P(('dp', 'cls')), may hold values from 0 to 127
Outputs:
- best: float32 [16384], P(('dp', 'cls'))
- assigned: float32 [16384], P(('dp', 'cls'))
- class_sums: float32 [256, 64, 128], P('cls', 'dp')
- class_weights: float32 [256, 64], P('cls', 'dp')
Inputs may be any that keep to these rules, and one draw needn't show every extreme that they name: `class_ids`: every class is assigned to at least one particle.
All inputs are finite; a program needn't handle non-finite values.
Results may differ from a plain program's by a relative error of at most 0.0045.
Values may be sent and summed in bfloat16 or wider, within the bound.
A program may use at most 64 MiB of HBM per device.

v0:
```python
import math

import jax
import jax.numpy as jnp
from jax import lax
from jax.sharding import PartitionSpec as P

ROTATIONS = 36


def phase_table(modes, count):
    order = (
        jnp.arange(modes, dtype=jnp.int32)[:, None] * jnp.arange(count, dtype=jnp.int32)[None, :]
    )
    angle = (order % count).astype(jnp.float32) * (2.0 * math.pi / count)
    return jnp.concatenate([jnp.cos(angle), -jnp.sin(angle)], axis=0).astype(jnp.bfloat16)


def turn(images, ctf_rows, rot_ids, modes, count):
    order = jnp.arange(modes, dtype=jnp.int32)[None, :] * rot_ids[:, None] % count
    angle = order.astype(jnp.float32) * (2.0 * math.pi / count)
    cosine = jnp.cos(angle)[:, None, :]
    sine = jnp.sin(angle)[:, None, :]
    real = images[..., :modes].astype(jnp.float32)
    imag = images[..., modes:].astype(jnp.float32)
    weight = ctf_rows[:, :, None]
    return jnp.concatenate(
        [weight * (real * cosine - imag * sine), weight * (real * sine + imag * cosine)], axis=2
    ).astype(jnp.bfloat16)


def on_device(images, references, ctf, class_ids, rot_ids, group_ids):
    parts, cycles, width = images.shape
    modes = width // 2
    block = references.shape[0]
    groups = ctf.shape[0]
    total_classes = block * lax.axis_size("cls")
    highest = lax.Precision.HIGHEST
    phases = phase_table(modes, ROTATIONS)
    classes = class_ids[:, 0]
    group_hot = (group_ids[:, None] == jnp.arange(groups, dtype=jnp.int32)[None, :]).astype(
        jnp.float32
    )
    ctf_rows = jnp.dot(group_hot, ctf, precision=highest)
    weighted = (ctf_rows[:, :, None] * images.astype(jnp.float32)).astype(jnp.bfloat16)
    stacked = jnp.concatenate([weighted[..., :modes], weighted[..., modes:]], axis=1)
    rotation_hit = rot_ids[:, None] == jnp.arange(ROTATIONS, dtype=jnp.int32)[None, :]
    initial = (jnp.full((parts,), -1e30, jnp.float32), jnp.zeros((parts,), jnp.float32))
    piece = lax.all_gather(references, "cls", axis=0, tiled=True)
    span = math.gcd(piece.shape[0], block)
    pieces = piece.reshape(piece.shape[0] // span, span, cycles, width)

    def score_block(inner, refs):
        best_now, picked_now, first = inner
        real = refs[..., :modes]
        imag = refs[..., modes:]
        paired = jnp.concatenate(
            [jnp.concatenate([real, imag], axis=1), jnp.concatenate([imag, -real], axis=1)], axis=0
        )
        both = jnp.einsum("ikm,ckm->icm", stacked, paired, preferred_element_type=jnp.float32)
        cross = jnp.concatenate([both[:, :span], both[:, span:]], axis=2).astype(jnp.bfloat16)
        scores = jnp.einsum("icj,jr->icr", cross, phases, preferred_element_type=jnp.float32)
        class_hit = classes[:, None] == first + jnp.arange(span, dtype=jnp.int32)[None, :]
        hit = class_hit[:, :, None] & rotation_hit[:, None, :]
        best_now = jnp.maximum(best_now, jnp.max(scores, axis=(1, 2)))
        picked_now = picked_now + jnp.sum(jnp.where(hit, scores, jnp.float32(0.0)), axis=(1, 2))
        return ((best_now, picked_now, first + span), None)

    result, _ = lax.scan(score_block, (initial[0], initial[1], jnp.asarray(jnp.int32(0))), pieces)
    best = result[0]
    picked = result[1]
    turned = turn(images, ctf_rows, rot_ids, modes, ROTATIONS)
    class_hot = classes[:, None] == jnp.arange(total_classes, dtype=jnp.int32)[None, :]
    partial_value = jnp.einsum(
        "pc,pf->cf",
        class_hot.astype(jnp.bfloat16),
        turned.reshape(parts, -1),
        preferred_element_type=jnp.float32,
    ).reshape(total_classes, cycles, width)
    weight_part = jnp.einsum(
        "pc,pf->cf", class_hot.astype(jnp.float32), ctf_rows * ctf_rows, precision=highest
    )
    owned, owned_weights = (
        lax.psum_scatter(partial_value, "cls", scatter_dimension=0, tiled=True),
        lax.psum_scatter(weight_part, "cls", scatter_dimension=0, tiled=True),
    )
    sums, weights = (
        lax.psum_scatter(owned, "dp", scatter_dimension=1, tiled=True),
        lax.psum_scatter(owned_weights, "dp", scatter_dimension=1, tiled=True),
    )
    return (best, picked, sums, weights)


def solution(mesh):
    return jax.shard_map(
        on_device,
        mesh=mesh,
        in_specs=(
            P(("dp", "cls"), None, None),
            P("cls", None, None),
            P(),
            P(("dp", "cls"), None),
            P(("dp", "cls")),
            P(("dp", "cls")),
        ),
        out_specs=(P(("dp", "cls")), P(("dp", "cls")), P("cls", "dp", None), P("cls", "dp")),
        check_vma=False,
    )
```

profile of v0, /device:TPU:1, one launch (start us, length us, event | category | flops | bytes accessed | tf_op | source)
XLA Modules:
  0.0 273.3 jit_solution(8778784675310802303)
XLA Ops:
  8.8 1.7 fusion.24
  11.4 2.7 %fusion.17 = (bf16[64,64,64]{2,1,0:T(8,128)(2,1)S(1)}, bf16[64,64,64]{2,1,0:T(8,128)(2,1)S(1)}) fusion(f32[64,64]{1,0:T(8,128)S(1)} %get-tuple-element.234, f32[64,64]{1,0:T(8,128)S(1)} %get-tuple-element.233, f32[64,64]{1,0:T(8,128)S(1)} %fusion.37, bf16[64,64,128]{2,1,0:T(8,128)(2,1)} %param.8), kind=kLoop, calls=%fused_computation.31 | loop fusion | flops 3145728 | bytes 2146304 | tf_op jit(solution)/shard_map/convert.4
  14.8 4.6 %fusion.21 = f32[256,64,128]{2,0,1:T(8,128)} fusion(s32[64]{0:T(128)S(1)} %bitcast.49, bf16[8,8,64,128]{3,2,1,0:T(8,128)(2,1)S(1)} %bitcast.46), kind=kOutput, calls=%fused_computation.36 | convolution fusion | flops 268451840 | bytes 9437440 | tf_op jit(solution)/shard_map/pc,pf->cf/dot_general | solution.py:74
  20.7 2.9 %copy.21 = bf16[64,64,128]{1,0,2:T(8,128)(2,1)S(1)} copy(bf16[64,64,128]{2,1,0:T(8,128)(2,1)S(1)} %copy-done.1) | data formatting | bytes 2097152 | tf_op args[0]
  26.4 42.2 %reduce-scatter.9.cloned.1.call-done = f32[16,64]{1,0:T(8,128)} async-done(((f32[256,64]{1,0:T(8,128)}), f32[16,64]{1,0:T(8,128)}) %reduce-scatter.9.cloned.1.call-update) | async-done | bytes 4112 | tf_op jit(solution)/shard_map/reduce_scatter | solution.py:85
  68.6 33.6 %all-reduce = f32[16,64]{1,0:T(8,128)S(1)} all-reduce(f32[16,64]{1,0:T(8,128)} %reduce-scatter.9.cloned.1.call-done), channel_id=5, replica_groups=mesh['dp'=16,'cls'=16] {'dp'}, use_global_device_ids=true, to_apply=%region_7.8.clone | all-reduce | flops 1024 | bytes 8192
  103.0 37.7 %reduce-scatter.5.cloned.1.call-done = f32[16,64,128]{2,0,1:T(8,128)} async-done(((f32[256,64,128]{2,0,1:T(8,128)}), f32[16,64,128]{2,0,1:T(8,128)}) %reduce-scatter.5.cloned.1.call-update) | async-done | bytes 524304 | tf_op jit(solution)/shard_map/reduce_scatter | solution.py:84
  140.7 45.4 %all-gather.2.cloned.1.call-done = bf16[256,64,128]{2,1,0:T(8,128)(2,1)} async-done(((bf16[16,64,128]{2,1,0:T(8,128)(2,1)}), bf16[256,64,128]{2,1,0:T(8,128)(2,1)}) %all-gather.2.cloned.1.call-update) | async-done | bytes 4194320 | tf_op jit(solution)/shard_map/all_gather | solution.py:49
  186.1 79.2 %while.16 = (s32[]{:T(128)}, f32[64]{0:T(128)S(1)}, f32[64]{0:T(128)S(1)}, bf16[16,16,64,128]{3,2,1,0:T(8,128)(2,1)}, bf16[64,128,64]{1,0,2:T(8,128)(2,1)S(1)}, ...) while((s32[]{:T(128)}, f32[64]{0:T(128)S(1)}, ...), condition=%wide.region_3.4_spmd.clone, body=%wide.region_0.3_spmd.clone.sunk | while | flops 45567376 | bytes 5261587 | solution.py:69
  186.3 1.0 constant_dynamic-slice_fusion.3
  189.2 1.8 select_reduce_fusion.2
  191.2 1.0 constant_dynamic-slice_fusion.3
  194.2 1.8 select_reduce_fusion.2
  199.1 1.8 select_reduce_fusion.2
  204.1 1.8 select_reduce_fusion.2
  209.0 1.8 select_reduce_fusion.2
  214.0 1.8 select_reduce_fusion.2
  218.9 1.8 select_reduce_fusion.2
  220.9 1.0 constant_dynamic-slice_fusion.3
  223.9 1.8 select_reduce_fusion.2
  225.9 1.0 constant_dynamic-slice_fusion.3
  228.9 1.8 select_reduce_fusion.2
  230.8 1.0 constant_dynamic-slice_fusion.3
  233.8 1.8 select_reduce_fusion.2
  238.8 1.8 select_reduce_fusion.2
  243.7 1.8 select_reduce_fusion.2
  248.7 1.8 select_reduce_fusion.2
  253.6 1.8 select_reduce_fusion.2
  258.6 1.8 select_reduce_fusion.2
  260.5 1.0 constant_dynamic-slice_fusion.3
  263.5 1.8 select_reduce_fusion.2
  265.4 1.4 copy.24
  (206 shorter events, 50.9 us)
Async XLA Ops:
  7.2 0.8 copy-start
  7.2 61.4 %reduce-scatter.9.cloned.1.call-start = ((), (), s32[]{:S(2)}) async-start(), calls=%async_computation.6 | async-start | bytes 139264 | tf_op jit(solution)/shard_map/reduce_scatter | solution.py:85
  10.5 130.2 %reduce-scatter.5.cloned.1.call-start = ((), (), s32[]{:S(2)}) async-start(), calls=%async_computation.4 | async-start | bytes 8912896 | tf_op jit(solution)/shard_map/reduce_scatter | solution.py:84
  14.2 0.7 copy-start.2
  19.4 1.2 copy-start.1
  19.5 4.1 %copy-start.6 = (u32[256]{0:T(256)S(1)}, u32[256]{0:T(256)}, u32[]{:S(2)}) copy-start(u32[256]{0:T(256)} %constant.65) | copy-start | bytes 3076
  19.5 166.6 %all-gather.2.cloned.1.call-start = ((), (), s32[]{:S(2)}) async-start(), calls=%async_computation.3 | async-start | bytes 4456448 | tf_op jit(solution)/shard_map/all_gather | solution.py:49
  20.2 245.1 %reduce-scatter.7.cloned.1.call-start = ((), (), s32[]{:S(2)}) async-start(), calls=%async_computation.5 | async-start | bytes 557056 | tf_op jit(solution)/shard_map/reduce_scatter | solution.py:88
  25.8 160.3 %copy-start.3 = (s32[64]{0:T(128)S(1)}, s32[64]{0:T(128)}, u32[]{:S(2)}) copy-start(s32[64]{0:T(128)} %param.12) | copy-start | bytes 772
  265.3 1.4 copy-start.4
  265.3 1.4 copy-start.5
Sparse Core Ops, SparseCore 0:
  10.6 57.9 reduce-scatter.8
  71.2 69.4 reduce-scatter.4
  142.5 43.5 all-gather.1
  189.4 75.0 reduce-scatter.6
where the time goes:
time: 274 us; the launch traced here: 273 us
  waiting for transfers between devices  126 us (46%)
  matrix products  46.8 us (17%)
  local copies, waits for them, and re-layouts  39.6 us (14%)
  blocking collectives  33.6 us (12%)
  between operations  14.6 us (5%)
  other arithmetic  11 us (4%)
    all_gather x1, waiting for transfers between devices, on_device(): piece = lax.all_gather(references, 'cls', axis=0, tiled=True)  45.4 us
    reduce_scatter x1, waiting for transfers between devices, on_device(): lax.psum_scatter(weight_part, 'cls', scatter_dimension=0, tiled=True)  42.2 us
    reduce_scatter x1, waiting for transfers between devices, on_device(): lax.psum_scatter(partial_value, 'cls', scatter_dimension=0, tiled=True)  37.7 us
    unnamed x1, blocking collectives  33.6 us
    dot_general x16, matrix products, score_block(): jnp.einsum('icj,jr->icr', cross, phases, preferred_element_type=jnp.float32)  28.3 us
    dynamic_slice x32, local copies, waits for them, and re-layouts, on_device(): lax.scan(score_block, (initial[0], initial[1], jnp.asarray(jnp.int32(0)))...  22.5 us
    dot_general x16, matrix products, score_block(): jnp.einsum('ikm,ckm->icm', stacked, paired, preferred_element_type=jnp.fl...  11.4 us
    concatenate x16, local copies, waits for them, and re-layouts, score_block(): jnp.concatenate([both[:, :span], both[:, span:]], axis=2)  9.5 us
  transfers between devices with their start and end apart: 4, of which 3 were waited for; matrix products, arithmetic and copies ran while one was open for 34% of the time, Pallas kernels for 0%

commit v1 on v0

v1 whole, which is shorter than its diff:
```python
import functools
import math

import jax
import jax.numpy as jnp
import numpy as np
from jax import lax
from jax.experimental import pallas as pl
from jax.experimental.pallas import tpu as pltpu
from jax.sharding import PartitionSpec as P

ROT = 36
HALF = ROT // 2
QUART = ROT // 4
CORES = 2
F32 = jnp.float32
BF16 = jnp.bfloat16
I32 = jnp.int32
MESH = pl.DeviceIdType.MESH
HIGHEST = lax.Precision.HIGHEST


def bf16_value(x):
    return float(np.float32(x).astype(BF16))


def turn_table(modes):
    order = (np.arange(ROT)[:, None] * np.arange(modes)[None, :]) % ROT
    angle = order * (2.0 * math.pi / ROT)
    cos, sin = np.cos(angle), np.sin(angle)
    table = np.zeros((64, 4 * modes), np.float32)
    table[:ROT] = np.concatenate([cos, cos, -sin, sin], axis=1)
    return table


def weighted_sum(terms):
    groups = {}
    for coefficient, value in terms:
        size = round(abs(coefficient), 12)
        if size < 1e-9:
            continue
        groups.setdefault(size, []).append((coefficient > 0, value))
    total = None
    for size, members in groups.items():
        part = None
        for positive, value in members:
            if part is None:
                part = value if positive else -value
            else:
                part = part + value if positive else part - value
        if size != 1.0:
            part = part * F32(bf16_value(size))
        total = part if total is None else total + part
    return total


def rotation_scores(re, im, modes):
    fold_re, fold_im = [None] * ROT, [None] * ROT
    for m in range(modes):
        for fold, part in ((fold_re, re), (fold_im, im)):
            at = m % ROT
            fold[at] = part(m) if fold[at] is None else fold[at] + part(m)
    even = [None] * (HALF + 1)
    odd = [None] * (HALF + 1)
    even[0], even[HALF] = fold_re[0], fold_re[HALF]
    for m in range(1, HALF):
        even[m] = fold_re[m] + fold_re[ROT - m]
        odd[m] = fold_im[m] - fold_im[ROT - m]
    scores = {}
    for r in range(QUART + 1):
        cos = lambda m: math.cos(2.0 * math.pi * ((m * r) % ROT) / ROT)
        sin = lambda m: math.sin(2.0 * math.pi * ((m * r) % ROT) / ROT)
        ce = weighted_sum([(cos(m), even[m]) for m in range(0, HALF + 1, 2)])
        co = weighted_sum([(cos(m), even[m]) for m in range(1, HALF + 1, 2)])
        se = weighted_sum([(sin(m), odd[m]) for m in range(2, HALF, 2)])
        so = weighted_sum([(sin(m), odd[m]) for m in range(1, HALF, 2)])
        if r == 0:
            scores[0], scores[HALF] = ce + co, ce - co
        elif r == QUART:
            scores[r], scores[ROT - r] = ce - so, ce + so
        else:
            plus, minus, both, apart = ce + co, ce - co, se + so, se - so
            scores[r], scores[ROT - r] = plus - both, plus + both
            scores[HALF - r], scores[HALF + r] = minus + apart, minus - apart
    return scores


def kernel(
    dims,
    tab_ref, img_ref, refs_ref, ctft_ref, cid_ref, rid_ref, gid_ref,
    best_ref, asg_ref, sums_ref, wts_ref,
    img_rx, ids_tx, ids_rx, xs, s2, rhs, s3, slots, xm, cts, tail, a_tx, a_rx,
    hot, wrow, facc, wacc, p_tx, p_rx, r_tx, r_rx, fin, finw, best_acc, asg_acc, e_tx, e_rx,
    ag_s, ag_r, aa_s, aa_r, rs_s, rs_r, one_s, one_r,
):
    ny, nx, nz, pd, cy, modes, cd = dims
    ndp, width, ncls = ny * nx, 2 * modes, nz * CORES * cd
    kd = cy // ndp
    hops, half = nz // 2, modes // 2
    rows = kd * pd
    dp, cls = lax.axis_index("dp"), lax.axis_index("cls")
    z, core = cls // CORES, cls % CORES
    y, x = dp // nx, dp % nx
    partner = (dp, z * CORES + 1 - core)

    def z_peer(step):
        return (dp, ((z + step + nz) % nz) * CORES + core)

    def dp_peer(step):
        return ((y + step // nx) % ny) * nx + (x + step % nx) % nx

    def remote(src, dst, send, recv, device):
        return pltpu.make_async_remote_copy(
            src_ref=src, dst_ref=dst, send_sem=send, recv_sem=recv, device_id=device, device_id_type=MESH
        )

    barrier = pltpu.get_barrier_semaphore()
    pl.semaphore_signal(barrier, inc=1, device_id=partner, device_id_type=MESH)
    for step in range(1, nz):
        pl.semaphore_signal(barrier, inc=1, device_id=z_peer(step), device_id_type=MESH)

    def greet(step, carry):
        pl.semaphore_signal(barrier, inc=1, device_id=(dp_peer(step), cls), device_id_type=MESH)
        return carry

    lax.fori_loop(1, ndp, greet, 0)

    ids_tx[...] = jnp.zeros_like(ids_tx)
    ids_tx[0:1, 0:pd] = cid_ref[...]
    ids_tx[1:2, 0:pd] = rid_ref[...]
    ids_tx[2:3, 0:pd] = gid_ref[...]
    pl.semaphore_wait(barrier, nz + ndp - 1)
    img_copy = remote(img_ref, img_rx, one_s.at[0], one_r.at[0], partner)
    ids_copy = remote(ids_tx, ids_rx, one_s.at[1], one_r.at[1], partner)

    lane_k = lax.broadcasted_iota(I32, (modes, 2 * cy), 1)

    def ref_pair(p, carry):
        both = refs_ref[pl.ds(2 * p, 2)].astype(F32).reshape(2 * cy, width)
        turned = both.T
        re, im = turned[:modes], turned[modes:]
        s3[pl.ds(pl.multiple_of(2 * p * modes, modes), modes), :] = jnp.where(lane_k < cy, re, pltpu.roll(im, cy, 1))
        s3[pl.ds(pl.multiple_of((2 * p + 1) * modes, modes), modes), :] = jnp.where(
            lane_k < cy, pltpu.roll(re, cy, 1), im
        )
        return carry

    lax.fori_loop(0, cd // 2, ref_pair, 0)

    def ag(way, hop, part):
        src = 0 if hop == 0 else 2 * hop - 1 + way
        dst = nz - 1 if hop == hops - 1 else 2 * hop + 1 + way
        span = pl.ds(part * half, half)
        return remote(
            slots.at[src, span], slots.at[dst, span], ag_s.at[way, hop, part], ag_r.at[way, hop, part],
            z_peer(1 - 2 * way),
        )

    def ag_sent(way, hop, part):
        return hop < hops - 1 or part == way

    def ref_mode(m, carry):
        slots[0, m] = s3[pl.ds(m, cd, stride=modes), :].astype(BF16)
        return carry

    for part in range(2):
        lax.fori_loop(part * half, (part + 1) * half, ref_mode, 0)
        for way in range(2):
            if ag_sent(way, 0, part):
                ag(way, 0, part).start()
    ids_copy.start()
    img_copy.start()

    def fill(base, image, groups):
        hot_g = (lax.broadcasted_iota(I32, (ctft_ref.shape[1], 2 * pd), 0) == groups).astype(F32)
        weights = jnp.dot(ctft_ref[...], hot_g, precision=HIGHEST, preferred_element_type=F32)

        def body(block, carry):
            for u in range(8):
                at = block * 8 + u
                start = pl.multiple_of((base + at) * cy, cy)
                xs[pl.ds(start, cy), :] = image[at].astype(F32) * carry[:, u : u + 1]
            return pltpu.roll(carry, 2 * pd - 8, 1)

        lax.fori_loop(0, pd // 8, body, weights)
        return weights

    cts[...] = fill(0, img_ref, ids_tx[2:3, :])

    eye = lax.broadcasted_iota(I32, (pd, 2 * pd), 0) == lax.broadcasted_iota(I32, (pd, 2 * pd), 1)
    rot_col = jnp.sum(jnp.where(eye, ids_tx[1:2, :].astype(F32), 0.0), axis=1, keepdims=True)
    rot_hot = (lax.broadcasted_iota(I32, (pd, 64), 1).astype(F32) == rot_col).astype(F32)
    table = jnp.dot(rot_hot, tab_ref[...], precision=HIGHEST, preferred_element_type=F32)
    cosine, sine = table[:, :width], table[:, width:]
    tail[...] = jnp.zeros_like(tail)
    lane_p = lax.broadcasted_iota(I32, (1, 2 * pd), 1)
    tail[2 * kd : 2 * kd + 1, :] = jnp.where(lane_p < pd, ids_tx[0:1, :].astype(F32), 0.0)

    def turn_to(step, target):
        first = dp_peer(step) * kd
        for k in range(kd):
            row = xs[pl.ds(first + k, pd, stride=cy), :]
            spun = row * cosine + pltpu.roll(row, modes, 1) * sine
            target[step, k * pd : (k + 1) * pd, :] = spun.astype(BF16)
            weight = cts[pl.ds(first + k, 1), :]
            square = jnp.where(lane_p < pd, weight * weight, 0.0)
            high = square.astype(BF16).astype(F32)
            tail[k : k + 1, :] = high
            tail[kd + k : kd + k + 1, :] = square - high
        target[step, rows : rows + 16, :] = tail[...].astype(BF16)

    def a2a(step):
        return remote(a_tx.at[step], a_rx.at[step], aa_s.at[step], aa_r.at[step], (dp_peer(step), cls))

    def send_turned(step, carry):
        turn_to(step, a_tx)
        a2a(step).start()
        return carry

    lax.fori_loop(1, ndp, send_turned, 0)
    turn_to(0, a_rx)

    ids_copy.wait_recv()
    img_copy.wait_recv()
    fill(pd, img_rx, ids_rx[2:3, :])

    def flip(k, carry):
        s2[pl.ds(pl.multiple_of(k * width, width), width), :] = xs[pl.ds(k, 2 * pd, stride=cy), :].T
        return carry

    lax.fori_loop(0, cy, flip, 0, unroll=2)

    def spread(m, carry):
        re = s2[pl.ds(m, cy, stride=width), :]
        im = s2[pl.ds(m + modes, cy, stride=width), :]
        rhs[m, 0:cy, 0 : 2 * pd] = re.astype(BF16)
        rhs[m, 0:cy, 2 * pd : 4 * pd] = (-im).astype(BF16)
        rhs[m, cy : 2 * cy, 0 : 2 * pd] = im.astype(BF16)
        rhs[m, cy : 2 * cy, 2 * pd : 4 * pd] = re.astype(BF16)
        return carry

    lax.fori_loop(0, modes, spread, 0, unroll=2)

    lane2 = lax.broadcasted_iota(I32, (8, 2 * pd), 1)
    ids_all = jnp.where(lane2 < pd, ids_tx[...], pltpu.roll(ids_rx[...], pd, 1))
    class_row, rot_row = ids_all[0:1, :], ids_all[1:2, :]
    best_acc[...] = jnp.full_like(best_acc, -1e30)
    asg_acc[...] = jnp.zeros_like(asg_acc)
    sub8 = lax.broadcasted_iota(I32, (8, 2 * pd), 0)

    def score(first, count):
        high = count * cd

        def cross(m, carry):
            left = slots[first : first + count, m].reshape(high, 2 * cy)
            xm[m, 0:high, :] = jnp.dot(left, rhs[m], preferred_element_type=F32)
            return carry

        lax.fori_loop(0, modes, cross, 0, unroll=8)

        def column(col, carry):
            at = pl.multiple_of(col * 8, 8)
            slot = first + at // cd
            hop = (slot + 1) // 2
            source = (z + jnp.where(slot % 2 == 1, -hop, hop) + nz) % nz
            base = (source * CORES + core) * cd + at % cd
            re = lambda m: xm[m, pl.ds(at, 8), 0 : 2 * pd]
            im = lambda m: xm[m, pl.ds(at, 8), 2 * pd : 4 * pd]
            scores = rotation_scores(re, im, modes)
            top, chosen = None, jnp.zeros((8, 2 * pd), F32)
            for r, value in scores.items():
                top = value if top is None else jnp.maximum(top, value)
                chosen = jnp.where(rot_row == r, value, chosen)
            best_acc[...] = jnp.maximum(best_acc[...], top)
            asg_acc[...] = asg_acc[...] + jnp.where(class_row == base + sub8, chosen, 0.0)
            return carry

        lax.fori_loop(0, high // 8, column, 0)

    done = 0
    for hop in range(1, hops):
        for part in range(2):
            for way in range(2):
                if ag_sent(way, hop, part):
                    ag(way, hop - 1, part).wait_recv()
                    ag(way, hop, part).start()
                elif hop < hops - 1:
                    ag(way, hop - 1, part).wait_recv()
        if hop < hops - 1:
            score(done, 2 * hop + 1 - done)
            done = 2 * hop + 1

    def arrived(step, carry):
        a2a(step).wait_recv()
        return carry

    lax.fori_loop(1, ndp, arrived, 0)
    class_iota = lax.broadcasted_iota(I32, (ncls, 2 * pd), 0).astype(F32)
    for q in range(ndp // 2):
        near = a_rx[2 * q, rows : rows + 16, :].astype(F32)
        far = a_rx[2 * q + 1, rows : rows + 16, :].astype(F32)
        both = near + pltpu.roll(far, pd, 1)
        hot[:, q * 2 * pd : (q + 1) * 2 * pd] = (class_iota == both[2 * kd : 2 * kd + 1, :]).astype(F32).astype(BF16)
        wrow[:, q * 2 * pd : (q + 1) * 2 * pd] = both.astype(BF16)

    def sum_cycle(k, carry):
        right = a_rx[:, pl.ds(pl.multiple_of(k * pd, pd), pd), :].reshape(ndp * pd, width)
        facc[k] = jnp.dot(hot[...], right, preferred_element_type=F32)
        return carry

    lax.fori_loop(0, kd, sum_cycle, 0)
    wacc[...] = jnp.zeros_like(wacc)
    wacc[:, 0:16] = lax.dot_general(hot[...], wrow[...], (((1,), (1,)), ((), ())), preferred_element_type=F32)

    def block_of(owner):
        at = pl.ds(pl.multiple_of(owner * cd, cd), cd)
        return [facc[k, at, :] for k in range(kd)], wacc[at, :]

    def put(target, index, values, weights):
        for k in range(kd):
            target[index, k * cd : (k + 1) * cd, :] = values[k].astype(BF16)
        high = weights.astype(BF16)
        target[index, kd * cd : (kd + 1) * cd, :] = high
        target[index, (kd + 1) * cd : (kd + 2) * cd, :] = (weights - high.astype(F32)).astype(BF16)

    def take(source, index):
        values = [source[index, k * cd : (k + 1) * cd, :].astype(F32) for k in range(kd)]
        high = source[index, kd * cd : (kd + 1) * cd, :].astype(F32)
        return values, high + source[index, (kd + 1) * cd : (kd + 2) * cd, :].astype(F32)

    def pack(chip, carry):
        put(p_tx, chip, *block_of(chip * CORES + 1 - core))
        return carry

    lax.fori_loop(0, nz, pack, 0)
    p_copy = remote(p_tx, p_rx, one_s.at[2], one_r.at[2], partner)
    p_copy.start()
    p_copy.wait_recv()

    def chip_sum(step):
        chip = (z + step) % nz
        values, weights = block_of(chip * CORES + core)
        more, more_w = take(p_rx, chip)
        return [a + b for a, b in zip(values, more)], weights + more_w

    def rs(step):
        return remote(r_tx.at[step], r_rx.at[step], rs_s.at[step], rs_r.at[step], z_peer(step))

    def send_sums(step, carry):
        put(r_tx, step, *chip_sum(step))
        rs(step).start()
        return carry

    lax.fori_loop(1, nz, send_sums, 0)
    values, weights = chip_sum(0)
    for k in range(kd):
        fin[k] = values[k]
    finw[...] = weights

    for part in range(2):
        for way in range(2):
            if not ag_sent(way, hops - 1, part):
                ag(way, hops - 2, part).wait_recv()
    for way in range(2):
        ag(way, hops - 1, way).wait_recv()
    score(done, nz - done)

    e_tx[...] = jnp.zeros_like(e_tx)
    e_tx[0:1, :] = jnp.max(best_acc[...], axis=0, keepdims=True)
    e_tx[1:2, :] = jnp.sum(asg_acc[...], axis=0, keepdims=True)
    e_copy = remote(e_tx, e_rx, one_s.at[3], one_r.at[3], partner)
    e_copy.start()

    def reduced(step, carry):
        rs(step).wait_recv()
        more, more_w = take(r_rx, step)
        for k in range(kd):
            fin[k] = fin[k] + more[k]
        finw[...] = finw[...] + more_w
        return carry

    lax.fori_loop(1, nz, reduced, 0)
    for k in range(kd):
        sums_ref[:, k, :] = fin[k]
    wts_ref[...] = finw[:, 0:kd] + finw[:, kd : 2 * kd]

    e_copy.wait_recv()
    other = pltpu.roll(e_rx[...], pd, 1)
    best_ref[...] = jnp.maximum(e_tx[0:1, :], other[0:1, :])[:, 0:pd]
    asg_ref[...] = (e_tx[1:2, :] + other[1:2, :])[:, 0:pd]

    for hop in range(hops):
        for part in range(2):
            for way in range(2):
                if ag_sent(way, hop, part):
                    ag(way, hop, part).wait_send()

    def left_dp(step, carry):
        a2a(step).wait_send()
        return carry

    def left_z(step, carry):
        rs(step).wait_send()
        return carry

    lax.fori_loop(1, ndp, left_dp, 0)
    lax.fori_loop(1, nz, left_z, 0)
    for copy in (img_copy, ids_copy, p_copy, e_copy):
        copy.wait_send()


def on_device(dims, images, references, ctf, class_ids, rot_ids, group_ids):
    ny, nx, nz, pd, cy, modes, cd = dims
    ndp, width, ncls = ny * nx, 2 * modes, nz * CORES * cd
    kd = cy // ndp
    hops = nz // 2
    block = kd * pd + 16
    reduce_rows = (kd + 2) * cd
    most = max(nz - 2 * (hops - 2) - 1 if hops > 2 else nz, 3 if hops > 2 else 0) * cd
    row = lambda ids: ids.reshape(1, pd)
    vmem = pl.BlockSpec(memory_space=pltpu.VMEM)
    dma = pltpu.SemaphoreType.DMA
    best, assigned, sums, weights = pl.pallas_call(
        functools.partial(kernel, dims),
        out_shape=(
            jax.ShapeDtypeStruct((1, pd), F32),
            jax.ShapeDtypeStruct((1, pd), F32),
            jax.ShapeDtypeStruct((cd, kd, width), F32),
            jax.ShapeDtypeStruct((cd, kd), F32),
        ),
        in_specs=[vmem] * 7,
        out_specs=(vmem,) * 4,
        scratch_shapes=[
            pltpu.VMEM((pd, cy, width), BF16),
            pltpu.VMEM((8, 2 * pd), I32),
            pltpu.VMEM((8, 2 * pd), I32),
            pltpu.VMEM((2 * pd * cy, width), F32),
            pltpu.VMEM((cy * width, 2 * pd), F32),
            pltpu.VMEM((modes, 2 * cy, 4 * pd), BF16),
            pltpu.VMEM((cd * modes, 2 * cy), F32),
            pltpu.VMEM((nz, modes, cd, 2 * cy), BF16),
            pltpu.VMEM((modes, most, 4 * pd), F32),
            pltpu.VMEM((cy, 2 * pd), F32),
            pltpu.VMEM((16, 2 * pd), F32),
            pltpu.VMEM((ndp, block, width), BF16),
            pltpu.VMEM((ndp, block, width), BF16),
            pltpu.VMEM((ncls, ndp * pd), BF16),
            pltpu.VMEM((16, ndp * pd), BF16),
            pltpu.VMEM((kd, ncls, width), F32),
            pltpu.VMEM((ncls, width), F32),
            pltpu.VMEM((nz, reduce_rows, width), BF16),
            pltpu.VMEM((nz, reduce_rows, width), BF16),
            pltpu.VMEM((nz, reduce_rows, width), BF16),
            pltpu.VMEM((nz, reduce_rows, width), BF16),
            pltpu.VMEM((kd, cd, width), F32),
            pltpu.VMEM((cd, width), F32),
            pltpu.VMEM((8, 2 * pd), F32),
            pltpu.VMEM((8, 2 * pd), F32),
            pltpu.VMEM((8, 2 * pd), F32),
            pltpu.VMEM((8, 2 * pd), F32),
            dma((2, hops, 2)),
            dma((2, hops, 2)),
            dma((ndp,)),
            dma((ndp,)),
            dma((nz,)),
            dma((nz,)),
            dma((4,)),
            dma((4,)),
        ],
        compiler_params=pltpu.CompilerParams(
            collective_id=0, has_side_effects=True, vmem_limit_bytes=60 * 1024 * 1024
        ),
    )(
        jnp.asarray(turn_table(modes)), images, references, ctf.T, row(class_ids), row(rot_ids), row(group_ids)
    )
    return best.reshape(pd), assigned.reshape(pd), sums, weights


def plane(count):
    side = 1
    while side * side < count:
        side *= 2
    return count // side, side


def solution(mesh):
    ndp, ncl = mesh.shape["dp"], mesh.shape["cls"]
    ny, nx = plane(ndp)

    def step(images, references, ctf, class_ids, rot_ids, group_ids):
        pd, cy, width = images.shape
        dims = (ny, nx, ncl // CORES, pd, cy, width // 2, references.shape[0])
        return on_device(dims, images, references, ctf, class_ids, rot_ids, group_ids)

    both = P(("dp", "cls"))
    return jax.shard_map(
        step,
        mesh=mesh,
        in_specs=(P(("dp", "cls"), None, None), P("cls", None, None), P(), P(("dp", "cls"), None), both, both),
        out_specs=(both, both, P("cls", "dp", None), P("cls", "dp")),
        check_vma=False,
    )
```

time: 274 us -> 58 us (0.21)
  waiting for transfers between devices: 126 us -> 0 us
  Pallas kernels: 0 us -> 53.2 us
  matrix products: 46.8 us -> 0 us
  local copies, waits for them, and re-layouts: 39.6 us -> 3.85 us
  blocking collectives: 33.6 us -> 0 us
  between operations: 14.6 us -> 0.65 us
  other arithmetic: 11 us -> 0 us
    reduce_scatter x3 -> x0, waiting for transfers between devices: 79.9 us -> none  [the longest x1 42.2 us: on_device(): lax.psum_scatter(weight_part, 'cls', scatter_dimension=0, tiled=True)]
    pallas_call x0 -> x1, Pallas kernels: none -> 53.2 us  [on_device(): pl.pallas_call(functools.partial(kernel, dims), out_shape=(jax.ShapeDtype...]
    dot_general x35 -> x0, matrix products: 46.8 us -> none  [the longest x16 28.3 us: score_block(): jnp.einsum('icj,jr->icr', cross, phases, preferred_element_type=jnp.float32)]
    all_gather x1 -> x0, waiting for transfers between devices: 45.4 us -> none  [on_device(): piece = lax.all_gather(references, 'cls', axis=0, tiled=True)]
    unnamed x1 -> x0, blocking collectives: 33.6 us -> none
    dynamic_slice x32 -> x0, local copies, waits for them, and re-layouts: 22.5 us -> none  [on_device(): lax.scan(score_block, (initial[0], initial[1], jnp.asarray(jnp.int32(0)))...]
    concatenate x16 -> x0, local copies, waits for them, and re-layouts: 9.5 us -> none  [score_block(): jnp.concatenate([both[:, :span], both[:, span:]], axis=2)]
    concatenate x19 -> x0, other arithmetic: 2.95 us -> none  [the longest x16 1.7 us: score_block(): jnp.concatenate([both[:, :span], both[:, span:]], axis=2)]
  transfers between devices with their start and end apart: 4 -> 0, of which waited for: 3 -> 0; matrix products, arithmetic and copies ran while one was open for 34% -> 0% of each run, Pallas kernels for 0% -> 0%
where the time goes in v1:
time: 58 us; the launch traced here: 57.7 us
  Pallas kernels  53.2 us (92%)
  local copies, waits for them, and re-layouts  3.85 us (7%)
  between operations  0.65 us (1%)
    pallas_call x1, Pallas kernels, on_device(): pl.pallas_call(functools.partial(kernel, dims), out_shape=(jax.ShapeDtype...  53.2 us
    unnamed x10, local copies, waits for them, and re-layouts  3.85 us

profile of v1, /device:TPU:1, one launch (start us, length us, event | category | flops | bytes accessed | tf_op | source)
XLA Modules:
  0.0 57.7 jit_solution(12459785747818261069)
XLA Ops:
  0.6 53.2 %shard_map.102 = (f32[1,64]{1,0:T(1,128)}, f32[1,64]{1,0:T(1,128)}, f32[16,4,128]{2,1,0:T(4,128)}, f32[16,4]{1,0:T(8,128)}) custom-call(f32[64,256]{1,0:T(8,128)} %constant.2.clone.tab_ref, bf16[64,64,128]{2,1,0:T(8,128)(2,1)} %img_ref.1, bf16[16,64,128]{2,1,0:T(8,128)(2,1)} %refs_ref.1, f32[64,128]{1,0:T(8,128)} %bitcast.6, s32[1,64]{1,0:T(1,128)} %bitcast.7, ...), custom_call_target="tpu_custom_call" | custom-call | tf_op jit(solution)/shard_map/pallas_call | solution.py:423
  53.9 0.0 copy-start
  53.9 0.7 %copy-done = f32[16,4]{1,0:T(8,128)S(1)} copy-done((f32[16,4]{1,0:T(8,128)S(1)}, f32[16,4]{1,0:T(8,128)}, u32[]{:S(2)}) %copy-start) | copy-done | bytes 280
  54.6 0.0 copy-start.2
  54.6 0.7 %copy.11 = f32[16,4]{0,1:T(4,128)} copy(f32[16,4]{1,0:T(8,128)S(1)} %copy-done) | data formatting | bytes 512
  55.2 0.0 copy-done.2
  55.3 0.0 copy-start.1
  55.3 0.5 copy.15
  55.8 0.1 copy-done.1
  55.9 0.5 copy.16
  56.4 1.4 %copy.17 = f32[16,4,128]{2,1,0:T(4,128)} copy(f32[16,4,128]{2,1,0:T(4,128)} %get-tuple-element.22) | data formatting | bytes 65536
Async XLA Ops:
  53.9 0.7 %copy-start = (f32[16,4]{1,0:T(8,128)S(1)}, f32[16,4]{1,0:T(8,128)}, u32[]{:S(2)}) copy-start(f32[16,4]{1,0:T(8,128)} %get-tuple-element.15) | copy-start | bytes 772
  54.6 0.7 %copy-start.2 = (f32[1,64]{1,0:T(1,128)S(1)}, f32[1,64]{1,0:T(1,128)}, u32[]{:S(2)}) copy-start(f32[1,64]{1,0:T(1,128)} %get-tuple-element.8) | copy-start | bytes 772
  55.3 0.6 %copy-start.1 = (f32[1,64]{1,0:T(1,128)S(1)}, f32[1,64]{1,0:T(1,128)}, u32[]{:S(2)}) copy-start(f32[1,64]{1,0:T(1,128)} %get-tuple-element.9) | copy-start | bytes 772

commit v2 on v1

v2 whole, which is shorter than its diff:
```python
import functools
import math

import jax
import jax.numpy as jnp
import numpy as np
from jax import lax
from jax.experimental import pallas as pl
from jax.experimental.pallas import tpu as pltpu
from jax.sharding import PartitionSpec as P

ROT = 36
HALF = ROT // 2
QUART = ROT // 4
CORES = 2
F32 = jnp.float32
BF16 = jnp.bfloat16
I32 = jnp.int32
MESH = pl.DeviceIdType.MESH
HIGHEST = lax.Precision.HIGHEST


def bf16_value(x):
    return float(np.float32(x).astype(BF16))


def turn_table(modes):
    order = (np.arange(ROT)[:, None] * np.arange(modes)[None, :]) % ROT
    angle = order * (2.0 * math.pi / ROT)
    cos, sin = np.cos(angle), np.sin(angle)
    table = np.zeros((64, 4 * modes), np.float32)
    table[:ROT] = np.concatenate([cos, cos, -sin, sin], axis=1)
    return table


def weighted_sum(terms):
    groups = {}
    for coefficient, value in terms:
        size = round(abs(coefficient), 12)
        if size < 1e-9:
            continue
        groups.setdefault(size, []).append((coefficient > 0, value))
    total = None
    for size, members in groups.items():
        part = None
        for positive, value in members:
            if part is None:
                part = value if positive else -value
            else:
                part = part + value if positive else part - value
        if size != 1.0:
            part = part * F32(bf16_value(size))
        total = part if total is None else total + part
    return total


def rotation_scores(re, im, modes):
    fold_re, fold_im = [None] * ROT, [None] * ROT
    for m in range(modes):
        for fold, part in ((fold_re, re), (fold_im, im)):
            at = m % ROT
            fold[at] = part(m) if fold[at] is None else fold[at] + part(m)
    even = [None] * (HALF + 1)
    odd = [None] * (HALF + 1)
    even[0], even[HALF] = fold_re[0], fold_re[HALF]
    for m in range(1, HALF):
        even[m] = fold_re[m] + fold_re[ROT - m]
        odd[m] = fold_im[m] - fold_im[ROT - m]
    scores = {}
    for r in range(QUART + 1):
        cos = lambda m: math.cos(2.0 * math.pi * ((m * r) % ROT) / ROT)
        sin = lambda m: math.sin(2.0 * math.pi * ((m * r) % ROT) / ROT)
        ce = weighted_sum([(cos(m), even[m]) for m in range(0, HALF + 1, 2)])
        co = weighted_sum([(cos(m), even[m]) for m in range(1, HALF + 1, 2)])
        se = weighted_sum([(sin(m), odd[m]) for m in range(2, HALF, 2)])
        so = weighted_sum([(sin(m), odd[m]) for m in range(1, HALF, 2)])
        if r == 0:
            scores[0], scores[HALF] = ce + co, ce - co
        elif r == QUART:
            scores[r], scores[ROT - r] = ce - so, ce + so
        else:
            plus, minus, both, apart = ce + co, ce - co, se + so, se - so
            scores[r], scores[ROT - r] = plus - both, plus + both
            scores[HALF - r], scores[HALF + r] = minus + apart, minus - apart
    return scores


def kernel(
    dims,
    tab_ref, img_ref, refs_ref, ctft_ref, cid_ref, rid_ref, gid_ref,
    out_ref,
    img_rx, ids_tx, ids_rx, xs, s2, rhs, s3, slots, xm, cts, tail, a_tx, a_rx,
    hot, wrow, facc, wacc, p_tx, p_rx, r_tx, r_rx, best_acc, asg_acc, e_tx, e_rx,
    ag_s, ag_r, aa_s, aa_r, pt_s, pt_r, rs_s, rs_r, one_s, one_r,
):
    ny, nx, nz, pd, cy, modes, cd = dims
    ndp, width, ncls = ny * nx, 2 * modes, nz * CORES * cd
    kd = cy // ndp
    hops, half = nz // 2, modes // 2
    px, pk, pm = cy + 1, width + 1, modes + 1
    dp, cls = lax.axis_index("dp"), lax.axis_index("cls")
    z, core = cls // CORES, cls % CORES
    y, x = dp // nx, dp % nx
    partner = (dp, z * CORES + 1 - core)

    def z_peer(step):
        return (dp, ((z + step + nz) % nz) * CORES + core)

    def dp_peer(step):
        return ((y + step // nx) % ny) * nx + (x + step % nx) % nx

    def remote(src, dst, send, recv, device):
        return pltpu.make_async_remote_copy(
            src_ref=src, dst_ref=dst, send_sem=send, recv_sem=recv, device_id=device, device_id_type=MESH
        )

    barrier = pltpu.get_barrier_semaphore()
    pl.semaphore_signal(barrier, inc=1, device_id=partner, device_id_type=MESH)
    for step in range(1, nz):
        pl.semaphore_signal(barrier, inc=1, device_id=z_peer(step), device_id_type=MESH)

    def greet(step, carry):
        pl.semaphore_signal(barrier, inc=1, device_id=(dp_peer(step), cls), device_id_type=MESH)
        return carry

    lax.fori_loop(1, ndp, greet, 0)

    ids_tx[...] = jnp.zeros_like(ids_tx)
    ids_tx[0:1, 0:pd] = cid_ref[...]
    ids_tx[1:2, 0:pd] = rid_ref[...]
    ids_tx[2:3, 0:pd] = gid_ref[...]
    pl.semaphore_wait(barrier, nz + ndp - 1)
    img_copy = remote(img_ref, img_rx, one_s.at[0], one_r.at[0], partner)
    ids_copy = remote(ids_tx, ids_rx, one_s.at[1], one_r.at[1], partner)

    lane_k = lax.broadcasted_iota(I32, (modes, 2 * cy), 1)

    def ref_pair(p, carry):
        both = refs_ref[pl.ds(2 * p, 2)].astype(F32).reshape(2 * cy, width)
        turned = both.T
        re, im = turned[:modes], turned[modes:]
        s3[pl.ds(2 * p * pm, modes), :] = jnp.where(lane_k < cy, re, pltpu.roll(im, cy, 1))
        s3[pl.ds((2 * p + 1) * pm, modes), :] = jnp.where(
            lane_k < cy, pltpu.roll(re, cy, 1), im
        )
        return carry

    lax.fori_loop(0, cd // 2, ref_pair, 0, unroll=4)

    def ag(way, hop, part):
        src = 0 if hop == 0 else 2 * hop - 1 + way
        dst = nz - 1 if hop == hops - 1 else 2 * hop + 1 + way
        span = pl.ds(part * half, half)
        return remote(
            slots.at[src, span], slots.at[dst, span], ag_s.at[way, hop, part], ag_r.at[way, hop, part],
            z_peer(1 - 2 * way),
        )

    def ag_sent(way, hop, part):
        return hop < hops - 1 or part == way

    def ref_mode(m, carry):
        slots[0, m] = s3[pl.ds(m, cd, stride=pm), :].astype(BF16)
        return carry

    for part in range(2):
        lax.fori_loop(part * half, (part + 1) * half, ref_mode, 0, unroll=8)
        for way in range(2):
            if ag_sent(way, 0, part):
                ag(way, 0, part).start()
    ids_copy.start()
    img_copy.start()

    def fill(base, image, groups):
        hot_g = (lax.broadcasted_iota(I32, (ctft_ref.shape[1], 2 * pd), 0) == groups).astype(F32)
        weights = jnp.dot(ctft_ref[...], hot_g, precision=HIGHEST, preferred_element_type=F32)

        def body(block, carry):
            for u in range(8):
                at = block * 8 + u
                xs[pl.ds((base + at) * px, cy), :] = image[at].astype(F32) * carry[:, u : u + 1]
            return pltpu.roll(carry, 2 * pd - 8, 1)

        lax.fori_loop(0, pd // 8, body, weights)
        return weights

    cts[...] = fill(0, img_ref, ids_tx[2:3, :])

    eye = lax.broadcasted_iota(I32, (pd, 2 * pd), 0) == lax.broadcasted_iota(I32, (pd, 2 * pd), 1)
    rot_col = jnp.sum(jnp.where(eye, ids_tx[1:2, :].astype(F32), 0.0), axis=1, keepdims=True)
    rot_hot = (lax.broadcasted_iota(I32, (pd, 64), 1).astype(F32) == rot_col).astype(F32)
    table = jnp.dot(rot_hot, tab_ref[...], precision=HIGHEST, preferred_element_type=F32)
    cosine, sine = table[:, :width], table[:, width:]
    tail[...] = jnp.zeros_like(tail)
    lane_p = lax.broadcasted_iota(I32, (1, 2 * pd), 1)
    tail[2 * kd : 2 * kd + 1, :] = jnp.where(lane_p < pd, ids_tx[0:1, :].astype(F32), 0.0)

    def turn_to(k, step, target):
        cycle = dp_peer(step) * kd + k
        row = xs[pl.ds(cycle, pd, stride=px), :]
        spun = row * cosine + pltpu.roll(row, modes, 1) * sine
        target[step, 16 + k * pd : 16 + (k + 1) * pd, :] = spun.astype(BF16)
        if k == 0:
            for at in range(kd):
                weight = cts[pl.ds(cycle + at, 1), :]
                square = jnp.where(lane_p < pd, weight * weight, 0.0)
                high = square.astype(BF16).astype(F32)
                tail[at : at + 1, :] = high
                tail[kd + at : kd + at + 1, :] = square - high
            target[step, 0:16, :] = tail[...].astype(BF16)

    def a2a(k, step):
        span = pl.ds(0, 16 + pd) if k == 0 else pl.ds(16 + k * pd, pd)
        return remote(
            a_tx.at[step, span], a_rx.at[step, span], aa_s.at[k, step], aa_r.at[k, step], (dp_peer(step), cls)
        )

    for k in range(kd):

        def send_turned(step, carry):
            turn_to(k, step, a_tx)
            a2a(k, step).start()
            return carry

        lax.fori_loop(1, ndp, send_turned, 0)
        turn_to(k, 0, a_rx)

    def forward(hop, part):
        for way in range(2):
            if ag_sent(way, hop, part):
                ag(way, hop - 1, part).wait_recv()
                ag(way, hop, part).start()
            elif hop < hops - 1:
                ag(way, hop - 1, part).wait_recv()

    ids_copy.wait_recv()
    img_copy.wait_recv()
    fill(pd, img_rx, ids_rx[2:3, :])
    forward(1, 0)

    def flip(k, carry):
        s2[pl.ds(k * pk, width), :] = xs[pl.ds(k, 2 * pd, stride=px), :].T
        return carry

    lax.fori_loop(0, cy, flip, 0, unroll=4)

    def spread(m, carry):
        re = s2[pl.ds(m, cy, stride=pk), :]
        im = s2[pl.ds(m + modes, cy, stride=pk), :]
        rhs[m, 0:cy, 0 : 2 * pd] = re.astype(BF16)
        rhs[m, 0:cy, 2 * pd : 4 * pd] = (-im).astype(BF16)
        rhs[m, cy : 2 * cy, 0 : 2 * pd] = im.astype(BF16)
        rhs[m, cy : 2 * cy, 2 * pd : 4 * pd] = re.astype(BF16)
        return carry

    lax.fori_loop(0, modes, spread, 0, unroll=4)
    forward(1, 1)

    lane2 = lax.broadcasted_iota(I32, (8, 2 * pd), 1)
    ids_all = jnp.where(lane2 < pd, ids_tx[...], pltpu.roll(ids_rx[...], pd, 1))
    class_row, rot_row = ids_all[0:1, :], ids_all[1:2, :]
    best_acc[...] = jnp.full_like(best_acc, -1e30)
    asg_acc[...] = jnp.zeros_like(asg_acc)
    sub8 = lax.broadcasted_iota(I32, (8, 2 * pd), 0)

    def score(first, count):
        high = count * cd

        def cross(m, carry):
            left = slots[first : first + count, m].reshape(high, 2 * cy)
            xm[m, 0:high, :] = jnp.dot(left, rhs[m], preferred_element_type=F32)
            return carry

        lax.fori_loop(0, modes, cross, 0, unroll=32)

        def column(col, carry):
            at = pl.multiple_of(col * 8, 8)
            slot = first + at // cd
            hop = (slot + 1) // 2
            source = (z + jnp.where(slot % 2 == 1, -hop, hop) + nz) % nz
            base = (source * CORES + core) * cd + at % cd
            re = lambda m: xm[m, pl.ds(at, 8), 0 : 2 * pd]
            im = lambda m: xm[m, pl.ds(at, 8), 2 * pd : 4 * pd]
            scores = rotation_scores(re, im, modes)
            top, chosen = None, jnp.zeros((8, 2 * pd), F32)
            for r, value in scores.items():
                top = value if top is None else jnp.maximum(top, value)
                chosen = jnp.where(rot_row == r, value, chosen)
            best_acc[...] = jnp.maximum(best_acc[...], top)
            asg_acc[...] = asg_acc[...] + jnp.where(class_row == base + sub8, chosen, 0.0)
            return carry

        lax.fori_loop(0, high // 8, column, 0)

    def one_hot():
        class_iota = lax.broadcasted_iota(I32, (ncls, 2 * pd), 0).astype(F32)
        for q in range(ndp // 2):
            near = a_rx[2 * q, 0:16, :].astype(F32)
            both = near + pltpu.roll(a_rx[2 * q + 1, 0:16, :].astype(F32), pd, 1)
            at = slice(q * 2 * pd, (q + 1) * 2 * pd)
            hot[:, at] = (class_iota == both[2 * kd : 2 * kd + 1, :]).astype(F32).astype(BF16)
            wrow[:, at] = both.astype(BF16)
        wacc[...] = jnp.zeros_like(wacc)
        wacc[:, 0:16] = lax.dot_general(hot[...], wrow[...], (((1,), (1,)), ((), ())), preferred_element_type=F32)

    def tiles(k):
        return 2 * cd if k == 0 else cd

    def at_class(owner):
        return pl.ds(pl.multiple_of(owner * cd, cd), cd)

    def with_rest(weights):
        high = weights.astype(BF16).astype(F32)
        return (high + pltpu.roll(weights - high, 16, 1)).astype(BF16)

    def without_rest(block):
        block = block.astype(F32)
        return block + pltpu.roll(block, width - 16, 1)

    def to_partner(k):
        span = pl.ds(0, tiles(k))
        return remote(p_tx.at[k, :, span], p_rx.at[k, :, span], pt_s.at[k], pt_r.at[k], partner)

    def to_owner(k, step):
        span = pl.ds(0, tiles(k))
        return remote(
            r_tx.at[k, step, span], r_rx.at[k, step, span], rs_s.at[k, step], rs_r.at[k, step], z_peer(step)
        )

    def sum_cycle(k):
        def arrived(step, carry):
            a2a(k, step).wait_recv()
            return carry

        lax.fori_loop(1, ndp, arrived, 0)
        if k == 0:
            one_hot()
        right = a_rx[:, 16 + k * pd : 16 + (k + 1) * pd, :].reshape(ndp * pd, width)
        facc[k] = jnp.dot(hot[...], right, preferred_element_type=F32)

        def pack(chip, carry):
            at = at_class(chip * CORES + 1 - core)
            p_tx[k, chip, 0:cd, :] = facc[k, at, :].astype(BF16)
            if k == 0:
                p_tx[k, chip, cd : 2 * cd, :] = with_rest(wacc[at, :])
            return carry

        lax.fori_loop(0, nz, pack, 0)
        to_partner(k).start()

    def chip_cycle(k):
        to_partner(k).wait_recv()

        def chip_sum(step):
            chip = (z + step) % nz
            at = at_class(chip * CORES + core)
            values = facc[k, at, :] + p_rx[k, chip, 0:cd, :].astype(F32)
            return values, (wacc[at, :] + without_rest(p_rx[k, chip, cd : 2 * cd, :]) if k == 0 else None)

        def send_sums(step, carry):
            values, weights = chip_sum(step)
            r_tx[k, step, 0:cd, :] = values.astype(BF16)
            if k == 0:
                keep = lax.broadcasted_iota(I32, (cd, width), 1) < 16
                r_tx[k, step, cd : 2 * cd, :] = with_rest(jnp.where(keep, weights, 0.0))
            to_owner(k, step).start()
            return carry

        lax.fori_loop(1, nz, send_sums, 0)
        values, weights = chip_sum(0)
        out_ref[k * cd : (k + 1) * cd, :] = values
        if k == 0:
            out_ref[kd * cd : (kd + 1) * cd, :] = weights

    def owned_cycle(k):
        def reduced(step, carry):
            to_owner(k, step).wait_recv()
            at = slice(k * cd, (k + 1) * cd)
            out_ref[at, :] = out_ref[at, :] + r_rx[k, step, 0:cd, :].astype(F32)
            if k == 0:
                at = slice(kd * cd, (kd + 1) * cd)
                out_ref[at, :] = out_ref[at, :] + without_rest(r_rx[k, step, cd : 2 * cd, :])
            return carry

        lax.fori_loop(1, nz, reduced, 0)

    todo = []
    for k in range(kd):
        todo.append((sum_cycle, k))
        if k > 0:
            todo.append((chip_cycle, k - 1))
    todo.append((chip_cycle, kd - 1))

    def some(count):
        for _ in range(min(count, len(todo))):
            act, k = todo.pop(0)
            act(k)

    some(1)
    done = 0
    for hop in range(2, hops):
        score(done, 2 * hop - 1 - done)
        done = 2 * hop - 1
        forward(hop, 0)
        some(2)
        forward(hop, 1)

    for part in range(2):
        for way in range(2):
            if not ag_sent(way, hops - 1, part):
                ag(way, hops - 2, part).wait_recv()
    score(done, nz - 1 - done)
    some(len(todo))
    for way in range(2):
        ag(way, hops - 1, way).wait_recv()
    score(nz - 1, 1)

    e_tx[...] = jnp.zeros_like(e_tx)
    e_tx[0:1, :] = jnp.max(best_acc[...], axis=0, keepdims=True)
    e_tx[1:2, :] = jnp.sum(asg_acc[...], axis=0, keepdims=True)
    e_copy = remote(e_tx, e_rx, one_s.at[2], one_r.at[2], partner)
    e_copy.start()

    for k in range(kd):
        owned_cycle(k)

    e_copy.wait_recv()
    other = pltpu.roll(e_rx[...], pd, 1)
    low = (kd + 1) * cd
    out_ref[low : low + 1, :] = jnp.maximum(e_tx[0:1, :], other[0:1, :])
    out_ref[low + 1 : low + 2, :] = e_tx[1:2, :] + other[1:2, :]
    out_ref[low + 2 : low + 8, :] = jnp.zeros((6, width), F32)

    for hop in range(hops):
        for part in range(2):
            for way in range(2):
                if ag_sent(way, hop, part):
                    ag(way, hop, part).wait_send()

    for k in range(kd):

        def left_dp(step, carry):
            a2a(k, step).wait_send()
            return carry

        def left_z(step, carry):
            to_owner(k, step).wait_send()
            return carry

        lax.fori_loop(1, ndp, left_dp, 0)
        lax.fori_loop(1, nz, left_z, 0)
        to_partner(k).wait_send()
    for copy in (img_copy, ids_copy, e_copy):
        copy.wait_send()


def deliver(pd, cd, kd, packed_ref, best_ref, asg_ref, sums_ref, wts_ref):
    low = (kd + 1) * cd
    best_ref[...] = packed_ref[low : low + 1, 0:pd]
    asg_ref[...] = packed_ref[low + 1 : low + 2, 0:pd]
    for k in range(kd):
        sums_ref[:, k, :] = packed_ref[k * cd : (k + 1) * cd, :]
    weights = packed_ref[kd * cd : (kd + 1) * cd, :].T
    wts_ref[...] = weights[0:kd, :] + weights[kd : 2 * kd, :]


def on_device(dims, images, references, ctf, class_ids, rot_ids, group_ids):
    ny, nx, nz, pd, cy, modes, cd = dims
    ndp, width, ncls = ny * nx, 2 * modes, nz * CORES * cd
    kd = cy // ndp
    hops = nz // 2
    block = kd * pd + 16
    most = 3 * cd
    row = lambda ids: ids.reshape(1, pd)
    vmem = pl.BlockSpec(memory_space=pltpu.VMEM)
    dma = pltpu.SemaphoreType.DMA
    packed = pl.pallas_call(
        functools.partial(kernel, dims),
        out_shape=jax.ShapeDtypeStruct(((kd + 1) * cd + 8, width), F32),
        in_specs=[vmem] * 7,
        out_specs=vmem,
        scratch_shapes=[
            pltpu.VMEM((pd, cy, width), BF16),
            pltpu.VMEM((8, 2 * pd), I32),
            pltpu.VMEM((8, 2 * pd), I32),
            pltpu.VMEM((2 * pd * (cy + 1), width), F32),
            pltpu.VMEM((cy * (width + 1), 2 * pd), F32),
            pltpu.VMEM((modes, 2 * cy, 4 * pd), BF16),
            pltpu.VMEM((cd * (modes + 1), 2 * cy), F32),
            pltpu.VMEM((nz, modes, cd, 2 * cy), BF16),
            pltpu.VMEM((modes, most, 4 * pd), F32),
            pltpu.VMEM((cy, 2 * pd), F32),
            pltpu.VMEM((16, 2 * pd), F32),
            pltpu.VMEM((ndp, block, width), BF16),
            pltpu.VMEM((ndp, block, width), BF16),
            pltpu.VMEM((ncls, ndp * pd), BF16),
            pltpu.VMEM((16, ndp * pd), BF16),
            pltpu.VMEM((kd, ncls, width), F32),
            pltpu.VMEM((ncls, width), F32),
            pltpu.VMEM((kd, nz, 2 * cd, width), BF16),
            pltpu.VMEM((kd, nz, 2 * cd, width), BF16),
            pltpu.VMEM((kd, nz, 2 * cd, width), BF16),
            pltpu.VMEM((kd, nz, 2 * cd, width), BF16),
            pltpu.VMEM((8, 2 * pd), F32),
            pltpu.VMEM((8, 2 * pd), F32),
            pltpu.VMEM((8, 2 * pd), F32),
            pltpu.VMEM((8, 2 * pd), F32),
            dma((2, hops, 2)),
            dma((2, hops, 2)),
            dma((kd, ndp)),
            dma((kd, ndp)),
            dma((kd,)),
            dma((kd,)),
            dma((kd, nz)),
            dma((kd, nz)),
            dma((3,)),
            dma((3,)),
        ],
        compiler_params=pltpu.CompilerParams(
            collective_id=0, has_side_effects=True, vmem_limit_bytes=60 * 1024 * 1024
        ),
    )(
        jnp.asarray(turn_table(modes)), images, references, ctf.T, row(class_ids), row(rot_ids), row(group_ids)
    )
    best, assigned, sums, weights = pl.pallas_call(
        functools.partial(deliver, pd, cd, kd),
        out_shape=(
            jax.ShapeDtypeStruct((1, pd), F32),
            jax.ShapeDtypeStruct((1, pd), F32),
            jax.ShapeDtypeStruct((cd, kd, width), F32),
            jax.ShapeDtypeStruct((kd, cd), F32),
        ),
        in_specs=[vmem],
        out_specs=(vmem,) * 4,
    )(packed)
    return best.reshape(pd), assigned.reshape(pd), sums, weights.T


def plane(count):
    side = 1
    while side * side < count:
        side *= 2
    return count // side, side


def solution(mesh):
    ndp, ncl = mesh.shape["dp"], mesh.shape["cls"]
    ny, nx = plane(ndp)

    def step(images, references, ctf, class_ids, rot_ids, group_ids):
        pd, cy, width = images.shape
        dims = (ny, nx, ncl // CORES, pd, cy, width // 2, references.shape[0])
        return on_device(dims, images, references, ctf, class_ids, rot_ids, group_ids)

    both = P(("dp", "cls"))
    return jax.shard_map(
        step,
        mesh=mesh,
        in_specs=(P(("dp", "cls"), None, None), P("cls", None, None), P(), P(("dp", "cls"), None), both, both),
        out_specs=(both, both, P("cls", "dp", None), P("cls", "dp")),
        check_vma=False,
    )
```

time: 58 us -> 48.9 us (0.84)
  Pallas kernels: 53.2 us -> 48.1 us
  local copies, waits for them, and re-layouts: 3.85 us -> 0 us
    pallas_call x1 -> x2, Pallas kernels: 53.2 us -> 48.1 us  [the longest x1 46.6 us: on_device(): pl.pallas_call(functools.partial(kernel, dims), out_shape=jax.ShapeDtypeS...]
    unnamed x10 -> x0, local copies, waits for them, and re-layouts: 3.85 us -> none
where the time goes in v2:
time: 48.9 us; the launch traced here: 48.7 us
  Pallas kernels  48.1 us (98%)
  between operations  0.64 us (1%)
    pallas_call x1, Pallas kernels, on_device(): pl.pallas_call(functools.partial(kernel, dims), out_shape=jax.ShapeDtypeS...  46.6 us
    pallas_call x1, Pallas kernels, on_device(): pl.pallas_call(functools.partial(deliver, pd, cd, kd), out_shape=(jax.Sha...  1.44 us

profile of v2, /device:TPU:1, one launch (start us, length us, event | category | flops | bytes accessed | tf_op | source)
XLA Modules:
  0.0 48.7 jit_solution(4897072882925234956)
XLA Ops:
  0.6 46.6 %shard_map.102.packed_ref = f32[88,128]{1,0:T(8,128)} custom-call(f32[64,256]{1,0:T(8,128)} %constant.2.clone.tab_ref, bf16[64,64,128]{2,1,0:T(8,128)(2,1)} %img_ref.1, bf16[16,64,128]{2,1,0:T(8,128)(2,1)} %refs_ref.1, f32[64,128]{1,0:T(8,128)} %bitcast.7, s32[1,64]{1,0:T(1,128)} %bitcast.8, s32[1,64]{1,0:T(1,128)} %bitcast.9, s32[1,64]{1,0:T(1,128)} %bitcast.10), custom_call_target="tpu_custom_call" | custom-call | tf_op jit(solution)/shard_map/pallas_call | solution.py:477
  47.3 1.4 %shard_map.103 = (f32[1,64]{1,0:T(1,128)}, f32[1,64]{1,0:T(1,128)}, f32[16,4,128]{2,1,0:T(4,128)}, f32[4,16]{1,0:T(4,128)}) custom-call(f32[88,128]{1,0:T(8,128)} %shard_map.102.packed_ref), custom_call_target="tpu_custom_call" | custom-call | tf_op jit(solution)/shard_map/pallas_call | solution.py:525

commit v3 on v2

--- a/solution.py
+++ b/solution.py
@@ -87,11 +87,12 @@
 
 def kernel(
     dims,
+    tab_hbm, img_hbm, refs_hbm, ctft_hbm, cid_hbm, rid_hbm, gid_hbm,
+    out_ref,
     tab_ref, img_ref, refs_ref, ctft_ref, cid_ref, rid_ref, gid_ref,
-    out_ref,
     img_rx, ids_tx, ids_rx, xs, s2, rhs, s3, slots, xm, cts, tail, a_tx, a_rx,
     hot, wrow, facc, wacc, p_tx, p_rx, r_tx, r_rx, best_acc, asg_acc, e_tx, e_rx,
-    ag_s, ag_r, aa_s, aa_r, pt_s, pt_r, rs_s, rs_r, one_s, one_r,
+    ag_s, ag_r, aa_s, aa_r, pt_s, pt_r, rs_s, rs_r, one_s, one_r, in_s,
 ):
     ny, nx, nz, pd, cy, modes, cd = dims
     ndp, width, ncls = ny * nx, 2 * modes, nz * CORES * cd
@@ -114,6 +115,14 @@
             src_ref=src, dst_ref=dst, send_sem=send, recv_sem=recv, device_id=device, device_id_type=MESH
         )
 
+    fetches = []
+    for at, (source, target) in enumerate((
+        (refs_hbm, refs_ref), (cid_hbm, cid_ref), (rid_hbm, rid_ref), (gid_hbm, gid_ref),
+        (ctft_hbm, ctft_ref), (tab_hbm, tab_ref), (img_hbm, img_ref),
+    )):
+        fetches.append(pltpu.make_async_copy(source, target, in_s.at[at]))
+        fetches[-1].start()
+
     barrier = pltpu.get_barrier_semaphore()
     pl.semaphore_signal(barrier, inc=1, device_id=partner, device_id_type=MESH)
     for step in range(1, nz):
@@ -125,12 +134,13 @@
 
     lax.fori_loop(1, ndp, greet, 0)
 
+    for fetch in fetches[1:4]:
+        fetch.wait()
     ids_tx[...] = jnp.zeros_like(ids_tx)
     ids_tx[0:1, 0:pd] = cid_ref[...]
     ids_tx[1:2, 0:pd] = rid_ref[...]
     ids_tx[2:3, 0:pd] = gid_ref[...]
-    pl.semaphore_wait(barrier, nz + ndp - 1)
-    img_copy = remote(img_ref, img_rx, one_s.at[0], one_r.at[0], partner)
+    img_copy = remote(img_hbm, img_rx, one_s.at[0], one_r.at[0], partner)
     ids_copy = remote(ids_tx, ids_rx, one_s.at[1], one_r.at[1], partner)
 
     lane_k = lax.broadcasted_iota(I32, (modes, 2 * cy), 1)
@@ -145,6 +155,7 @@
         )
         return carry
 
+    fetches[0].wait()
     lax.fori_loop(0, cd // 2, ref_pair, 0, unroll=4)
 
     def ag(way, hop, part):
@@ -152,7 +163,7 @@
         dst = nz - 1 if hop == hops - 1 else 2 * hop + 1 + way
         span = pl.ds(part * half, half)
         return remote(
-            slots.at[src, span], slots.at[dst, span], ag_s.at[way, hop, part], ag_r.at[way, hop, part],
+            slots.at[src, span], slots.at[dst, span], ag_s.at[0], ag_r.at[2 * (2 * hop + part) + way],
             z_peer(1 - 2 * way),
         )
 
@@ -163,28 +174,32 @@
         slots[0, m] = s3[pl.ds(m, cd, stride=pm), :].astype(BF16)
         return carry
 
+    lax.fori_loop(0, modes, ref_mode, 0, unroll=8)
+
+    def fill(base, image, groups):
+        hot_g = (lax.broadcasted_iota(I32, (ctft_ref.shape[1], 2 * pd), 0) == groups).astype(F32)
+        weights = jnp.dot(ctft_ref[...], hot_g, precision=HIGHEST, preferred_element_type=F32)
+
+        def body(block, carry):
+            for u in range(8):
+                at = block * 8 + u
+                xs[pl.ds((base + at) * px, cy), :] = image[at].astype(F32) * carry[:, u : u + 1]
+            return pltpu.roll(carry, 2 * pd - 8, 1)
+
+        lax.fori_loop(0, pd // 8, body, weights)
+        return weights
+
+    for fetch in fetches[4:]:
+        fetch.wait()
+    cts[...] = fill(0, img_ref, ids_tx[2:3, :])
+
+    pl.semaphore_wait(barrier, nz + ndp - 1)
     for part in range(2):
-        lax.fori_loop(part * half, (part + 1) * half, ref_mode, 0, unroll=8)
         for way in range(2):
             if ag_sent(way, 0, part):
                 ag(way, 0, part).start()
     ids_copy.start()
     img_copy.start()
-
-    def fill(base, image, groups):
-        hot_g = (lax.broadcasted_iota(I32, (ctft_ref.shape[1], 2 * pd), 0) == groups).astype(F32)
-        weights = jnp.dot(ctft_ref[...], hot_g, precision=HIGHEST, preferred_element_type=F32)
-
-        def body(block, carry):
-            for u in range(8):
-                at = block * 8 + u
-                xs[pl.ds((base + at) * px, cy), :] = image[at].astype(F32) * carry[:, u : u + 1]
-            return pltpu.roll(carry, 2 * pd - 8, 1)
-
-        lax.fori_loop(0, pd // 8, body, weights)
-        return weights
-
-    cts[...] = fill(0, img_ref, ids_tx[2:3, :])
 
     eye = lax.broadcasted_iota(I32, (pd, 2 * pd), 0) == lax.broadcasted_iota(I32, (pd, 2 * pd), 1)
     rot_col = jnp.sum(jnp.where(eye, ids_tx[1:2, :].astype(F32), 0.0), axis=1, keepdims=True)
@@ -212,8 +227,13 @@
     def a2a(k, step):
         span = pl.ds(0, 16 + pd) if k == 0 else pl.ds(16 + k * pd, pd)
         return remote(
-            a_tx.at[step, span], a_rx.at[step, span], aa_s.at[k, step], aa_r.at[k, step], (dp_peer(step), cls)
+            a_tx.at[step, span], a_rx.at[step, span], aa_s.at[0], aa_r.at[k], (dp_peer(step), cls)
         )
+
+    def a2a_all(k):
+        span = pl.ds(0, 16 + pd) if k == 0 else pl.ds(16 + k * pd, pd)
+        peers = pl.ds(1, ndp - 1)
+        return remote(a_tx.at[peers, span], a_rx.at[peers, span], aa_s.at[0], aa_r.at[k], (dp_peer(1), cls))
 
     for k in range(kd):
 
@@ -222,7 +242,7 @@
             a2a(k, step).start()
             return carry
 
-        lax.fori_loop(1, ndp, send_turned, 0)
+        lax.fori_loop(1, ndp, send_turned, 0, unroll=5)
         turn_to(k, 0, a_rx)
 
     def forward(hop, part):
@@ -263,7 +283,7 @@
     asg_acc[...] = jnp.zeros_like(asg_acc)
     sub8 = lax.broadcasted_iota(I32, (8, 2 * pd), 0)
 
-    def score(first, count):
+    def score(first, count, between=None):
         high = count * cd
 
         def cross(m, carry):
@@ -314,7 +334,6 @@
         return (high + pltpu.roll(weights - high, 16, 1)).astype(BF16)
 
     def without_rest(block):
-        block = block.astype(F32)
         return block + pltpu.roll(block, width - 16, 1)
 
     def to_partner(k):
@@ -324,28 +343,25 @@
     def to_owner(k, step):
         span = pl.ds(0, tiles(k))
         return remote(
-            r_tx.at[k, step, span], r_rx.at[k, step, span], rs_s.at[k, step], rs_r.at[k, step], z_peer(step)
+            r_tx.at[k, step, span], r_rx.at[k, step, span], rs_s.at[k], rs_r.at[k], z_peer(step)
         )
 
+    def to_owner_all(k):
+        span, peers = pl.ds(0, tiles(k)), pl.ds(1, nz - 1)
+        return remote(r_tx.at[k, peers, span], r_rx.at[k, peers, span], rs_s.at[k], rs_r.at[k], z_peer(1))
+
     def sum_cycle(k):
-        def arrived(step, carry):
-            a2a(k, step).wait_recv()
-            return carry
-
-        lax.fori_loop(1, ndp, arrived, 0)
+        a2a_all(k).wait_recv()
         if k == 0:
             one_hot()
         right = a_rx[:, 16 + k * pd : 16 + (k + 1) * pd, :].reshape(ndp * pd, width)
         facc[k] = jnp.dot(hot[...], right, preferred_element_type=F32)
 
-        def pack(chip, carry):
+        for chip in range(nz):
             at = at_class(chip * CORES + 1 - core)
             p_tx[k, chip, 0:cd, :] = facc[k, at, :].astype(BF16)
             if k == 0:
                 p_tx[k, chip, cd : 2 * cd, :] = with_rest(wacc[at, :])
-            return carry
-
-        lax.fori_loop(0, nz, pack, 0)
         to_partner(k).start()
 
     def chip_cycle(k):
@@ -355,34 +371,29 @@
             chip = (z + step) % nz
             at = at_class(chip * CORES + core)
             values = facc[k, at, :] + p_rx[k, chip, 0:cd, :].astype(F32)
-            return values, (wacc[at, :] + without_rest(p_rx[k, chip, cd : 2 * cd, :]) if k == 0 else None)
-
-        def send_sums(step, carry):
+            return values, (wacc[at, :] + without_rest(p_rx[k, chip, cd : 2 * cd, :].astype(F32)) if k == 0 else None)
+
+        keep = lax.broadcasted_iota(I32, (cd, width), 1) < 16
+        for step in range(1, nz):
             values, weights = chip_sum(step)
             r_tx[k, step, 0:cd, :] = values.astype(BF16)
             if k == 0:
-                keep = lax.broadcasted_iota(I32, (cd, width), 1) < 16
                 r_tx[k, step, cd : 2 * cd, :] = with_rest(jnp.where(keep, weights, 0.0))
+        for step in sorted(range(1, nz), key=lambda step: -min(step, nz - step)):
             to_owner(k, step).start()
-            return carry
-
-        lax.fori_loop(1, nz, send_sums, 0)
         values, weights = chip_sum(0)
         out_ref[k * cd : (k + 1) * cd, :] = values
         if k == 0:
             out_ref[kd * cd : (kd + 1) * cd, :] = weights
 
     def owned_cycle(k):
-        def reduced(step, carry):
-            to_owner(k, step).wait_recv()
-            at = slice(k * cd, (k + 1) * cd)
-            out_ref[at, :] = out_ref[at, :] + r_rx[k, step, 0:cd, :].astype(F32)
-            if k == 0:
-                at = slice(kd * cd, (kd + 1) * cd)
-                out_ref[at, :] = out_ref[at, :] + without_rest(r_rx[k, step, cd : 2 * cd, :])
-            return carry
-
-        lax.fori_loop(1, nz, reduced, 0)
+        to_owner_all(k).wait_recv()
+        at = slice(k * cd, (k + 1) * cd)
+        out_ref[at, :] = out_ref[at, :] + sum(r_rx[k, step, 0:cd, :].astype(F32) for step in range(1, nz))
+        if k == 0:
+            at = slice(kd * cd, (kd + 1) * cd)
+            rest = sum(r_rx[k, step, cd : 2 * cd, :].astype(F32) for step in range(1, nz))
+            out_ref[at, :] = out_ref[at, :] + without_rest(rest)
 
     todo = []
     for k in range(kd):
@@ -405,12 +416,13 @@
         some(2)
         forward(hop, 1)
 
+    some(len(todo))
+
     for part in range(2):
         for way in range(2):
             if not ag_sent(way, hops - 1, part):
                 ag(way, hops - 2, part).wait_recv()
     score(done, nz - 1 - done)
-    some(len(todo))
     for way in range(2):
         ag(way, hops - 1, way).wait_recv()
     score(nz - 1, 1)
@@ -431,24 +443,12 @@
     out_ref[low + 1 : low + 2, :] = e_tx[1:2, :] + other[1:2, :]
     out_ref[low + 2 : low + 8, :] = jnp.zeros((6, width), F32)
 
-    for hop in range(hops):
-        for part in range(2):
-            for way in range(2):
-                if ag_sent(way, hop, part):
-                    ag(way, hop, part).wait_send()
-
+    gone = slots.at[pl.ds(0, nz - 1)]
+    remote(gone, gone, ag_s.at[0], ag_r.at[0], z_peer(1)).wait_send()
+    gone = pl.ds(1, ndp - 1)
+    remote(a_tx.at[gone], a_rx.at[gone], aa_s.at[0], aa_r.at[0], (dp_peer(1), cls)).wait_send()
     for k in range(kd):
-
-        def left_dp(step, carry):
-            a2a(k, step).wait_send()
-            return carry
-
-        def left_z(step, carry):
-            to_owner(k, step).wait_send()
-            return carry
-
-        lax.fori_loop(1, ndp, left_dp, 0)
-        lax.fori_loop(1, nz, left_z, 0)
+        to_owner_all(k).wait_send()
         to_partner(k).wait_send()
     for copy in (img_copy, ids_copy, e_copy):
         copy.wait_send()
@@ -477,9 +477,16 @@
     packed = pl.pallas_call(
         functools.partial(kernel, dims),
         out_shape=jax.ShapeDtypeStruct(((kd + 1) * cd + 8, width), F32),
-        in_specs=[vmem] * 7,
+        in_specs=[pl.BlockSpec(memory_space=pl.ANY)] * 7,
         out_specs=vmem,
         scratch_shapes=[
+            pltpu.VMEM((64, 2 * width), F32),
+            pltpu.VMEM((pd, cy, width), BF16),
+            pltpu.VMEM((cd, cy, width), BF16),
+            pltpu.VMEM((cy, ctf.shape[0]), F32),
+            pltpu.VMEM((1, pd), I32),
+            pltpu.VMEM((1, pd), I32),
+            pltpu.VMEM((1, pd), I32),
             pltpu.VMEM((pd, cy, width), BF16),
             pltpu.VMEM((8, 2 * pd), I32),
             pltpu.VMEM((8, 2 * pd), I32),
@@ -505,16 +512,17 @@
             pltpu.VMEM((8, 2 * pd), F32),
             pltpu.VMEM((8, 2 * pd), F32),
             pltpu.VMEM((8, 2 * pd), F32),
-            dma((2, hops, 2)),
-            dma((2, hops, 2)),
-            dma((kd, ndp)),
-            dma((kd, ndp)),
+            dma((1,)),
+            dma((4 * hops,)),
+            dma((1,)),
             dma((kd,)),
             dma((kd,)),
-            dma((kd, nz)),
-            dma((kd, nz)),
+            dma((kd,)),
+            dma((kd,)),
+            dma((kd,)),
             dma((3,)),
             dma((3,)),
+            dma((7,)),
         ],
         compiler_params=pltpu.CompilerParams(
             collective_id=0, has_side_effects=True, vmem_limit_bytes=60 * 1024 * 1024

time: 48.9 us -> 41.8 us (0.85)
  Pallas kernels: 48.1 us -> 41 us
    pallas_call x1, Pallas kernels: 46.6 us -> 39.6 us  [on_device(): pl.pallas_call(functools.partial(kernel, dims), out_shape=jax.ShapeDtypeS...]
where the time goes in v3:
time: 41.8 us; the launch traced here: 41.7 us
  Pallas kernels  41 us (98%)
  between operations  0.64 us (2%)
    pallas_call x1, Pallas kernels, on_device(): pl.pallas_call(functools.partial(kernel, dims), out_shape=jax.ShapeDtypeS...  39.6 us
    pallas_call x1, Pallas kernels, on_device(): pl.pallas_call(functools.partial(deliver, pd, cd, kd), out_shape=(jax.Sha...  1.44 us

profile of v3, /device:TPU:1, one launch (start us, length us, event | category | flops | bytes accessed | tf_op | source)
XLA Modules:
  0.0 41.7 jit_solution(18346913125377446600)
XLA Ops:
  0.6 39.6 %shard_map.102.packed_ref = f32[88,128]{1,0:T(8,128)} custom-call(f32[64,256]{1,0:T(8,128)} %constant.2.clone.tab_hbm, bf16[64,64,128]{2,1,0:T(8,128)(2,1)} %img_hbm.1, bf16[16,64,128]{2,1,0:T(8,128)(2,1)} %refs_hbm.1, f32[64,128]{1,0:T(8,128)} %bitcast.7, s32[1,64]{1,0:T(1,128)} %bitcast.8, s32[1,64]{1,0:T(1,128)} %bitcast.9, s32[1,64]{1,0:T(1,128)} %bitcast.10), custom_call_target="tpu_custom_call" | custom-call | tf_op jit(solution)/shard_map/pallas_call | solution.py:477
  40.2 1.4 %shard_map.103 = (f32[1,64]{1,0:T(1,128)}, f32[1,64]{1,0:T(1,128)}, f32[16,4,128]{2,1,0:T(4,128)}, f32[4,16]{1,0:T(4,128)}) custom-call(f32[88,128]{1,0:T(8,128)} %shard_map.102.packed_ref), custom_call_target="tpu_custom_call" | custom-call | tf_op jit(solution)/shard_map/pallas_call | solution.py:533

commit v4 on v3

--- a/solution.py
+++ b/solution.py
@@ -92,7 +92,7 @@
     tab_ref, img_ref, refs_ref, ctft_ref, cid_ref, rid_ref, gid_ref,
     img_rx, ids_tx, ids_rx, xs, s2, rhs, s3, slots, xm, cts, tail, a_tx, a_rx,
     hot, wrow, facc, wacc, p_tx, p_rx, r_tx, r_rx, best_acc, asg_acc, e_tx, e_rx,
-    ag_s, ag_r, aa_s, aa_r, pt_s, pt_r, rs_s, rs_r, one_s, one_r, in_s,
+    ag_s, ag_r, sd_r, aa_s, aa_r, pt_s, pt_r, rs_s, rs_r, one_s, one_r, in_s,
 ):
     ny, nx, nz, pd, cy, modes, cd = dims
     ndp, width, ncls = ny * nx, 2 * modes, nz * CORES * cd
@@ -158,17 +158,47 @@
     fetches[0].wait()
     lax.fori_loop(0, cd // 2, ref_pair, 0, unroll=4)
 
-    def ag(way, hop, part):
-        src = 0 if hop == 0 else 2 * hop - 1 + way
-        dst = nz - 1 if hop == hops - 1 else 2 * hop + 1 + way
-        span = pl.ds(part * half, half)
+    color = (x + y) % 2
+    quarter = modes // 4
+
+    def slot_of(way, hop):
+        return 0 if hop == 0 else nz - 1 if hop == hops else 2 * hop - 1 + way
+
+    def piece_at(piece):
+        return pl.ds(pl.multiple_of((color + piece // 2) % 2 * half + piece % 2 * quarter, quarter), quarter)
+
+    def ag(way, hop, piece):
+        at = 2 * piece + way if hop == 0 else 4 * (hop + 1) + 2 * piece + way
         return remote(
-            slots.at[src, span], slots.at[dst, span], ag_s.at[0], ag_r.at[2 * (2 * hop + part) + way],
-            z_peer(1 - 2 * way),
+            slots.at[slot_of(way, hop), piece_at(piece)], slots.at[slot_of(way, hop + 1), piece_at(piece)],
+            ag_s.at[0], ag_r.at[at], z_peer(1 - 2 * way),
         )
 
-    def ag_sent(way, hop, part):
-        return hop < hops - 1 or part == way
+    def start_both(piece):
+        for way in range(2):
+            ag(way, 0, piece).start()
+
+    def side(slot, axis):
+        to = ((y + (ny - 1) * axis) % ny) * nx + (x + (nx - 1) * (1 - axis)) % nx
+        ref = slots.at[slot, piece_at(axis)]
+        return remote(ref, ref, ag_s.at[1], sd_r.at[slot], (to, cls))
+
+    def complete(*wanted):
+        for slot in wanted:
+            ref = slots.at[slot, pl.ds(pl.multiple_of((color + 1) % 2 * half, half), half)]
+            remote(ref, ref, ag_s.at[1], sd_r.at[slot], partner).wait_recv()
+
+    def forward(hop, piece):
+        for way in range(2):
+            ag(way, hop - 1, piece).wait_recv()
+            if hop < hops - 1 or piece == way:
+                ag(way, hop, piece).start()
+            if hop > 1:
+                side(slot_of(way, hop), piece).start()
+
+    def forward_far(way):
+        ag(way, hops - 1, way).wait_recv()
+        side(nz - 1, way).start()
 
     def ref_mode(m, carry):
         slots[0, m] = s3[pl.ds(m, cd, stride=pm), :].astype(BF16)
@@ -194,10 +224,8 @@
     cts[...] = fill(0, img_ref, ids_tx[2:3, :])
 
     pl.semaphore_wait(barrier, nz + ndp - 1)
-    for part in range(2):
-        for way in range(2):
-            if ag_sent(way, 0, part):
-                ag(way, 0, part).start()
+    for piece in range(3):
+        start_both(piece)
     ids_copy.start()
     img_copy.start()
 
@@ -245,14 +273,6 @@
         lax.fori_loop(1, ndp, send_turned, 0, unroll=5)
         turn_to(k, 0, a_rx)
 
-    def forward(hop, part):
-        for way in range(2):
-            if ag_sent(way, hop, part):
-                ag(way, hop - 1, part).wait_recv()
-                ag(way, hop, part).start()
-            elif hop < hops - 1:
-                ag(way, hop - 1, part).wait_recv()
-
     ids_copy.wait_recv()
     img_copy.wait_recv()
     fill(pd, img_rx, ids_rx[2:3, :])
@@ -262,7 +282,10 @@
         s2[pl.ds(k * pk, width), :] = xs[pl.ds(k, 2 * pd, stride=px), :].T
         return carry
 
-    lax.fori_loop(0, cy, flip, 0, unroll=4)
+    lax.fori_loop(0, cy // 2, flip, 0, unroll=4)
+    forward(1, 1)
+    start_both(3)
+    lax.fori_loop(cy // 2, cy, flip, 0, unroll=4)
 
     def spread(m, carry):
         re = s2[pl.ds(m, cy, stride=pk), :]
@@ -274,7 +297,6 @@
         return carry
 
     lax.fori_loop(0, modes, spread, 0, unroll=4)
-    forward(1, 1)
 
     lane2 = lax.broadcasted_iota(I32, (8, 2 * pd), 1)
     ids_all = jnp.where(lane2 < pd, ids_tx[...], pltpu.roll(ids_rx[...], pd, 1))
@@ -292,6 +314,8 @@
             return carry
 
         lax.fori_loop(0, modes, cross, 0, unroll=32)
+        if between is not None:
+            between()
 
         def column(col, carry):
             at = pl.multiple_of(col * 8, 8)
@@ -408,23 +432,28 @@
             act(k)
 
     some(1)
-    done = 0
-    for hop in range(2, hops):
-        score(done, 2 * hop - 1 - done)
-        done = 2 * hop - 1
+    for hop in range(2, hops - 1):
         forward(hop, 0)
-        some(2)
         forward(hop, 1)
-
-    some(len(todo))
-
-    for part in range(2):
+    for piece in (2, 3):
         for way in range(2):
-            if not ag_sent(way, hops - 1, part):
-                ag(way, hops - 2, part).wait_recv()
-    score(done, nz - 1 - done)
-    for way in range(2):
-        ag(way, hops - 1, way).wait_recv()
+            ag(way, 0, piece).wait_recv()
+    last = hops - 1 if hops > 2 else None
+    score(0, 3, last and (lambda: forward(last, 0)))
+    if last:
+        forward(last, 1)
+    some(2)
+    for slot in range(3, nz - 3, 2):
+        complete(slot, slot + 1)
+        score(slot, 2)
+    forward_far(0)
+    some(len(todo) - 1)
+    forward_far(1)
+    some(1)
+    if last:
+        complete(nz - 3, nz - 2)
+        score(nz - 3, 2)
+    complete(nz - 1)
     score(nz - 1, 1)
 
     e_tx[...] = jnp.zeros_like(e_tx)
@@ -443,8 +472,10 @@
     out_ref[low + 1 : low + 2, :] = e_tx[1:2, :] + other[1:2, :]
     out_ref[low + 2 : low + 8, :] = jnp.zeros((6, width), F32)
 
-    gone = slots.at[pl.ds(0, nz - 1)]
+    gone = slots.at[pl.ds(0, nz), pl.ds(0, quarter * (4 * hops + 2) // nz)]
     remote(gone, gone, ag_s.at[0], ag_r.at[0], z_peer(1)).wait_send()
+    gone = slots.at[pl.ds(0, nz - 3), pl.ds(0, half)]
+    remote(gone, gone, ag_s.at[1], ag_r.at[0], z_peer(1)).wait_send()
     gone = pl.ds(1, ndp - 1)
     remote(a_tx.at[gone], a_rx.at[gone], aa_s.at[0], aa_r.at[0], (dp_peer(1), cls)).wait_send()
     for k in range(kd):
@@ -512,8 +543,9 @@
             pltpu.VMEM((8, 2 * pd), F32),
             pltpu.VMEM((8, 2 * pd), F32),
             pltpu.VMEM((8, 2 * pd), F32),
-            dma((1,)),
-            dma((4 * hops,)),
+            dma((2,)),
+            dma((4 * hops + 4,)),
+            dma((nz,)),
             dma((1,)),
             dma((kd,)),
             dma((kd,)),

time: 41.8 us -> 40.5 us (0.969)
  Pallas kernels: 41 us -> 39.7 us
    pallas_call x1, Pallas kernels: 39.6 us -> 38.2 us  [on_device(): pl.pallas_call(functools.partial(kernel, dims), out_shape=jax.ShapeDtypeS...]
where the time goes in v4:
time: 40.5 us; the launch traced here: 40.3 us
  Pallas kernels  39.7 us (98%)
  between operations  0.64 us (2%)
    pallas_call x1, Pallas kernels, on_device(): pl.pallas_call(functools.partial(kernel, dims), out_shape=jax.ShapeDtypeS...  38.2 us
    pallas_call x1, Pallas kernels, on_device(): pl.pallas_call(functools.partial(deliver, pd, cd, kd), out_shape=(jax.Sha...  1.44 us

profile of v4, /device:TPU:1, one launch (start us, length us, event | category | flops | bytes accessed | tf_op | source)
XLA Modules:
  0.0 40.3 jit_solution(2744052444586362741)
XLA Ops:
  0.6 38.2 %shard_map.102.packed_ref = f32[88,128]{1,0:T(8,128)} custom-call(f32[64,256]{1,0:T(8,128)} %constant.2.clone.tab_hbm, bf16[64,64,128]{2,1,0:T(8,128)(2,1)} %img_hbm.1, bf16[16,64,128]{2,1,0:T(8,128)(2,1)} %refs_hbm.1, f32[64,128]{1,0:T(8,128)} %bitcast.7, s32[1,64]{1,0:T(1,128)} %bitcast.8, s32[1,64]{1,0:T(1,128)} %bitcast.9, s32[1,64]{1,0:T(1,128)} %bitcast.10), custom_call_target="tpu_custom_call" | custom-call | tf_op jit(solution)/shard_map/pallas_call | solution.py:508
  38.9 1.4 %shard_map.103 = (f32[1,64]{1,0:T(1,128)}, f32[1,64]{1,0:T(1,128)}, f32[16,4,128]{2,1,0:T(4,128)}, f32[4,16]{1,0:T(4,128)}) custom-call(f32[88,128]{1,0:T(8,128)} %shard_map.102.packed_ref), custom_call_target="tpu_custom_call" | custom-call | tf_op jit(solution)/shard_map/pallas_call | solution.py:565

commit v5 on v4

--- a/solution.py
+++ b/solution.py
@@ -223,12 +223,6 @@
         fetch.wait()
     cts[...] = fill(0, img_ref, ids_tx[2:3, :])
 
-    pl.semaphore_wait(barrier, nz + ndp - 1)
-    for piece in range(3):
-        start_both(piece)
-    ids_copy.start()
-    img_copy.start()
-
     eye = lax.broadcasted_iota(I32, (pd, 2 * pd), 0) == lax.broadcasted_iota(I32, (pd, 2 * pd), 1)
     rot_col = jnp.sum(jnp.where(eye, ids_tx[1:2, :].astype(F32), 0.0), axis=1, keepdims=True)
     rot_hot = (lax.broadcasted_iota(I32, (pd, 64), 1).astype(F32) == rot_col).astype(F32)
@@ -252,6 +246,18 @@
                 tail[kd + at : kd + at + 1, :] = square - high
             target[step, 0:16, :] = tail[...].astype(BF16)
 
+    def turn_first(step, carry):
+        turn_to(0, step, a_tx)
+        return carry
+
+    lax.fori_loop(1, ndp, turn_first, 0, unroll=5)
+
+    pl.semaphore_wait(barrier, nz + ndp - 1)
+    for piece in range(3):
+        start_both(piece)
+    ids_copy.start()
+    img_copy.start()
+
     def a2a(k, step):
         span = pl.ds(0, 16 + pd) if k == 0 else pl.ds(16 + k * pd, pd)
         return remote(
@@ -266,7 +272,8 @@
     for k in range(kd):
 
         def send_turned(step, carry):
-            turn_to(k, step, a_tx)
+            if k > 0:
+                turn_to(k, step, a_tx)
             a2a(k, step).start()
             return carry
 
@@ -521,10 +528,10 @@
             pltpu.VMEM((pd, cy, width), BF16),
             pltpu.VMEM((8, 2 * pd), I32),
             pltpu.VMEM((8, 2 * pd), I32),
-            pltpu.VMEM((2 * pd * (cy + 1), width), F32),
-            pltpu.VMEM((cy * (width + 1), 2 * pd), F32),
+            pltpu.VMEM((2 * pd * (cy + 1) + cy, width), F32),
+            pltpu.VMEM((cy * (width + 1) + width, 2 * pd), F32),
             pltpu.VMEM((modes, 2 * cy, 4 * pd), BF16),
-            pltpu.VMEM((cd * (modes + 1), 2 * cy), F32),
+            pltpu.VMEM((cd * (modes + 1) + modes, 2 * cy), F32),
             pltpu.VMEM((nz, modes, cd, 2 * cy), BF16),
             pltpu.VMEM((modes, most, 4 * pd), F32),
             pltpu.VMEM((cy, 2 * pd), F32),

time: 40.5 us -> 39.8 us (0.983)
  Pallas kernels: 39.7 us -> 39 us
    pallas_call x1, Pallas kernels: 38.2 us -> 37.6 us  [on_device(): pl.pallas_call(functools.partial(kernel, dims), out_shape=jax.ShapeDtypeS...]
where the time goes in v5:
time: 39.8 us; the launch traced here: 39.7 us
  Pallas kernels  39 us (98%)
  between operations  0.64 us (2%)
    pallas_call x1, Pallas kernels, on_device(): pl.pallas_call(functools.partial(kernel, dims), out_shape=jax.ShapeDtypeS...  37.6 us
    pallas_call x1, Pallas kernels, on_device(): pl.pallas_call(functools.partial(deliver, pd, cd, kd), out_shape=(jax.Sha...  1.44 us

profile of v5, /device:TPU:1, one launch (start us, length us, event | category | flops | bytes accessed | tf_op | source)
XLA Modules:
  0.0 39.7 jit_solution(1740447649192077209)
XLA Ops:
  0.6 37.6 %shard_map.102.packed_ref = f32[88,128]{1,0:T(8,128)} custom-call(f32[64,256]{1,0:T(8,128)} %constant.2.clone.tab_hbm, bf16[64,64,128]{2,1,0:T(8,128)(2,1)} %img_hbm.1, bf16[16,64,128]{2,1,0:T(8,128)(2,1)} %refs_hbm.1, f32[64,128]{1,0:T(8,128)} %bitcast.7, s32[1,64]{1,0:T(1,128)} %bitcast.8, s32[1,64]{1,0:T(1,128)} %bitcast.9, s32[1,64]{1,0:T(1,128)} %bitcast.10), custom_call_target="tpu_custom_call" | custom-call | tf_op jit(solution)/shard_map/pallas_call | solution.py:515
  38.2 1.4 %shard_map.103 = (f32[1,64]{1,0:T(1,128)}, f32[1,64]{1,0:T(1,128)}, f32[16,4,128]{2,1,0:T(4,128)}, f32[4,16]{1,0:T(4,128)}) custom-call(f32[88,128]{1,0:T(8,128)} %shard_map.102.packed_ref), custom_call_target="tpu_custom_call" | custom-call | tf_op jit(solution)/shard_map/pallas_call | solution.py:572
